TPU v7x, 256 devices: a whole 4x4x8 slice. The times are simulated.
256 devices in a mesh: seq: 32 (over x, z), tp: 8 (over y, core).
Axes of the slice: x: 4, y: 4, z: 8, core: 2. Of those that a mesh axis runs over, the one named last changes fastest.
Arguments:
- event_vectors: bfloat16 [16384, 6144], P('seq'), may hold values from -6 to 6
- question_projector: bfloat16 [6144, 4096], P('seq', 'tp'), may hold values from -0.078125 to 0.078125
- lookup_projector: bfloat16 [6144, 4096], P('seq', 'tp'), may hold values from -0.078125 to 0.078125
- content_projector: bfloat16 [6144, 4096], P('seq', 'tp'), may hold values from -0.078125 to 0.078125
- channel_fading_speed: float32 [32], P('tp'), may hold values from 1.2207031e-05 to 0.03334
- surge_fading: float32 [16384], P('seq'), may hold values from -0.6932 to 0, as said below
- channel_scaling_coefficient: float32 [4096], P('tp'), may hold values from 0.1 to 1.9
- final_projector: bfloat16 [4096, 6144], P('seq', 'tp'), may hold values from -0.09375 to 0.09375
Outputs:
- mixed: bfloat16 [16384, 6144], P('seq', 'tp')
Inputs may be any that keep to these rules, and one draw needn't show every extreme that they name: `surge_fading`: zero at all but a few positions of the sequence.
All inputs are finite; a program needn't handle non-finite values.
Results may differ from a plain program's by a relative error of at most 0.0063.
Values may be sent and summed in bfloat16 or wider, within the bound.
A program may use at most 128 MiB of HBM per device.

v0:
```python
import jax
import jax.numpy as jnp
from jax import lax
from jax.sharding import PartitionSpec as P

HD = 128
SPAN_LENGTH = 512


def entering(part, axis, combine, identity):
    place = lax.axis_index(axis)
    gathered = jax.tree.map(lambda a: lax.all_gather(a, axis), part)
    state = jax.tree.map(lambda a, e: jnp.zeros_like(a) + jnp.asarray(e, a.dtype), part, identity)

    def one(step, state):
        return combine(
            state, jax.tree.map(lambda a: lax.dynamic_index_in_dim(a, step, 0, False), gathered)
        )

    return lax.fori_loop(0, place, one, state)


def block_pass(carry, inputs):
    carried, before = carry
    query_block, key_block, value_block, log_block = inputs
    inside = jnp.cumsum(log_block, axis=0)
    block_total = inside[-1]
    highest = lax.Precision.HIGHEST
    scores = jnp.einsum("thd,shd->hts", query_block, key_block, precision=highest)
    spread_log = inside.T[:, :, None] - inside.T[:, None, :]
    rows_index = lax.broadcasted_iota(jnp.int32, (SPAN_LENGTH, SPAN_LENGTH), 0)
    cols_index = lax.broadcasted_iota(jnp.int32, (SPAN_LENGTH, SPAN_LENGTH), 1)
    causal = (rows_index >= cols_index)[None, :, :]
    weight = jnp.where(causal, jnp.exp(jnp.where(causal, spread_log, 0.0)), 0.0)
    within = jnp.einsum("hts,shd->thd", scores * weight, value_block, precision=highest)
    across = jnp.einsum(
        "thd,hde->the", query_block * jnp.exp(inside)[:, :, None], carried, precision=highest
    )
    updated = jnp.exp(block_total)[:, None, None] * carried + jnp.einsum(
        "shd,she->hde",
        key_block * jnp.exp(block_total[None, :] - inside)[:, :, None],
        value_block,
        precision=highest,
    )
    factor = jnp.exp(before[None, :] + inside)
    return ((updated, before + block_total), (within + across, factor))


def chain_combine(earlier, later):
    return (earlier[0] + later[0], jnp.exp(later[0])[:, None, None] * earlier[1] + later[1])


def local(
    event_vectors,
    question_projector,
    lookup_projector,
    content_projector,
    channel_fading_speed,
    surge_fading,
    channel_scaling_coefficient,
    final_projector,
):
    tok_count = event_vectors.shape[0]
    number_of_heads = channel_fading_speed.shape[0]

    def project_rows(shard_rows):
        return jnp.dot(event_vectors, shard_rows, preferred_element_type=jnp.float32)

    query_sum = project_rows(lax.all_gather(question_projector, "seq", axis=0, tiled=True))
    key_sum = project_rows(lax.all_gather(lookup_projector, "seq", axis=0, tiled=True))
    value_sum = project_rows(lax.all_gather(content_projector, "seq", axis=0, tiled=True))
    queries = jax.nn.silu(query_sum).astype(jnp.bfloat16)
    keys_act = jax.nn.silu(key_sum).astype(jnp.bfloat16)
    values_act = value_sum.astype(jnp.bfloat16)
    span_count = tok_count // SPAN_LENGTH
    shaped = (span_count, SPAN_LENGTH, number_of_heads, HD)
    query_blocks = queries.astype(jnp.float32).reshape(shaped)
    key_blocks = keys_act.astype(jnp.float32).reshape(shaped)
    value_blocks = values_act.astype(jnp.float32).reshape(shaped)
    stepwise_fading_exponent = (surge_fading[:, None] - channel_fading_speed[None, :]).reshape(
        (span_count, SPAN_LENGTH, number_of_heads)
    )
    start = (
        jnp.zeros((number_of_heads, HD, HD), jnp.float32),
        jnp.zeros((number_of_heads,), jnp.float32),
    )
    (local_state, local_log), (outputs, factors) = lax.scan(
        block_pass, start, (query_blocks, key_blocks, value_blocks, stepwise_fading_exponent)
    )
    identity = (
        jnp.zeros((number_of_heads,), jnp.float32),
        jnp.zeros((number_of_heads, HD, HD), jnp.float32),
    )
    prior_log, incoming = entering((local_log, local_state), "seq", chain_combine, identity)
    query_flat = query_blocks.reshape((tok_count, number_of_heads, HD))
    reached = jnp.einsum("thd,hde->the", query_flat, incoming, precision=lax.Precision.HIGHEST)
    attention = (
        outputs.reshape((tok_count, number_of_heads, HD))
        + factors.reshape((tok_count, number_of_heads))[:, :, None] * reached
    )
    meansq = jnp.mean(attention * attention, axis=-1, keepdims=True)
    normed = (
        attention
        / jnp.sqrt(meansq + 1e-05)
        * channel_scaling_coefficient.reshape((number_of_heads, HD))[None, :, :]
    )
    normed = normed.reshape((tok_count, number_of_heads * HD)).astype(jnp.bfloat16)
    every_head = lax.all_gather(normed, "tp", axis=1, tiled=True)
    mixed = jnp.dot(
        every_head,
        lax.all_gather(final_projector, "seq", axis=0, tiled=True),
        preferred_element_type=jnp.float32,
    )
    return mixed.astype(jnp.bfloat16)


def solution(mesh):
    in_specs = (
        P("seq", None),
        P("seq", "tp"),
        P("seq", "tp"),
        P("seq", "tp"),
        P("tp"),
        P("seq"),
        P("tp"),
        P("seq", "tp"),
    )
    out_specs = P("seq", "tp")
    return jax.shard_map(local, mesh=mesh, in_specs=in_specs, out_specs=out_specs, check_vma=False)
```

profile of v0, /device:TPU:1, one launch (start us, length us, event | category | flops | bytes accessed | tf_op | source)
XLA Modules:
  0.0 514.1 jit_solution(17631043664003188020)
XLA Ops:
  6.5 0.0 all-gather.9.cloned.1.call-start
  6.5 0.7 all-gather.9.cloned.1.call-update
  7.3 0.0 all-gather.13.cloned.1.call-start
  7.3 0.7 all-gather.13.cloned.1.call-update
  8.0 0.0 all-gather.11.cloned.1.call-start
  8.1 0.7 all-gather.11.cloned.1.call-update
  8.7 0.0 all-gather.19.cloned.1.call-start
  8.8 0.8 broadcast_subtract_fusion
  9.6 1.2 reduce-window.6
  10.8 0.2 slice_reduce_fusion
  10.9 0.2 reduce-window.9
  11.1 0.1 add_bitcast_fusion
  11.2 0.2 slice_reduce_fusion.1
  11.4 0.1 subtract_exponential_fusion
  11.5 90.6 %all-gather.9.cloned.1.call-done = bf16[6144,512]{1,0:T(8,128)(2,1)} async-done(((bf16[192,512]{1,0:T(8,128)(2,1)}), bf16[6144,512]{1,0:T(8,128)(2,1)}) %all-gather.9.cloned.1.call-update) | async-done | bytes 6291472 | tf_op jit(solution)/shard_map/all_gather | solution.py:71
  102.1 8.1 %convolution_convert_fusion.1 = bf16[512,512]{0,1:T(8,128)(2,1)S(1)} fusion(bf16[512,6144]{1,0:T(8,128)(2,1)} %param.10, bf16[6144,512]{1,0:T(8,128)(2,1)} %all-gather.9.cloned.1.call-done), kind=kOutput, calls=%fused_computation.18 | convolution fusion | flops 3221487616 | bytes 13107200 | tf_op jit(solution)/shard_map/dot_general | solution.py:67
  110.2 80.2 %all-gather.13.cloned.1.call-done = bf16[6144,512]{1,0:T(8,128)(2,1)} async-done(((bf16[192,512]{1,0:T(8,128)(2,1)}), bf16[6144,512]{1,0:T(8,128)(2,1)}) %all-gather.13.cloned.1.call-update) | async-done | bytes 6291472 | tf_op jit(solution)/shard_map/all_gather | solution.py:70
  190.4 8.2 %multiply_convert_fusion.1 = bf16[512,512]{0,1:T(8,128)(2,1)S(1)} fusion(bf16[512,6144]{1,0:T(8,128)(2,1)} %param.10, bf16[6144,512]{1,0:T(8,128)(2,1)} %all-gather.13.cloned.1.call-done), kind=kOutput, calls=%fused_computation.27 | convolution fusion | flops 3222536192 | bytes 13107200 | tf_op jit(solution)/shard_map/dot_general | solution.py:67
  198.6 1.4 convolution_add_fusion.1
  199.9 0.0 all-gather.19.cloned.1.call-update
  200.0 0.0 all-gather.17.cloned.1.call-start
  200.0 0.5 all-gather.17.cloned.1.call-update
  200.6 0.0 all-gather.15.cloned.1.call-start
  200.6 31.6 %all-gather.1 = f32[32,1,4]{2,1,0:T(1,128)S(1)} all-gather(f32[1,1,4]{2,1,0:T(1,128)S(1)} %bitcast.69), channel_id=1, replica_groups=mesh['seq'=32,'tp'=8] {'seq'}, dimensions={0}, use_global_device_ids=true | all-gather | bytes 528 | tf_op jit(solution)/shard_map/all_gather | solution.py:12
  232.2 0.1 iota_compare_fusion
  232.3 46.4 %all-gather.11.cloned.1.call-done = bf16[6144,512]{1,0:T(8,128)(2,1)} async-done(((bf16[192,512]{1,0:T(8,128)(2,1)}), bf16[6144,512]{1,0:T(8,128)(2,1)}) %all-gather.11.cloned.1.call-update) | async-done | bytes 6291472 | tf_op jit(solution)/shard_map/all_gather | solution.py:69
  278.7 8.2 %multiply_convert_fusion.2 = bf16[512,512]{0,1:T(8,128)(2,1)S(1)} fusion(bf16[512,6144]{1,0:T(8,128)(2,1)} %param.10, bf16[6144,512]{1,0:T(8,128)(2,1)} %all-gather.11.cloned.1.call-done), kind=kOutput, calls=%fused_computation.28 | convolution fusion | flops 3222536192 | bytes 13107200 | tf_op jit(solution)/shard_map/dot_general | solution.py:67
  286.9 0.7 fusion.23
  287.6 3.7 fusion
  291.3 0.0 copy-start
  291.3 1.0 fusion.12
  292.4 84.0 %all-gather.19.cloned.1.call-done = f32[128,128,128]{2,1,0:T(8,128)} async-done(((f32[4,128,128]{2,1,0:T(8,128)}), f32[128,128,128]{2,1,0:T(8,128)}) %all-gather.19.cloned.1.call-update) | async-done | bytes 8388624 | tf_op jit(solution)/shard_map/all_gather | solution.py:12
  376.4 0.2 while.3
  376.6 0.7 multiply_reduce_fusion
  377.4 0.0 copy-done
  377.4 0.9 multiply_convert_fusion
  378.3 0.0 all-gather.15.cloned.1.call-update
  378.4 86.3 %all-gather.17.cloned.1.call-done = bf16[4096,768]{1,0:T(8,128)(2,1)} async-done(((bf16[128,768]{1,0:T(8,128)(2,1)}), bf16[4096,768]{1,0:T(8,128)(2,1)}) %all-gather.17.cloned.1.call-update) | async-done | bytes 6291472 | tf_op jit(solution)/shard_map/all_gather | solution.py:111
  464.6 34.2 %all-gather.15.cloned.1.call-done = bf16[512,4096]{0,1:T(8,128)(2,1)} async-done(((bf16[512,512]{0,1:T(8,128)(2,1)}), bf16[512,4096]{0,1:T(8,128)(2,1)}) %all-gather.15.cloned.1.call-update) | async-done | bytes 4194320 | tf_op jit(solution)/shard_map/all_gather | solution.py:108
  498.8 8.4 %convolution_convert_fusion = bf16[512,768]{1,0:T(8,128)(2,1)} fusion(bf16[512,4096]{0,1:T(8,128)(2,1)} %all-gather.15.cloned.1.call-done, bf16[4096,768]{1,0:T(8,128)(2,1)} %all-gather.17.cloned.1.call-done), kind=kOutput, calls=%fused_computation.12 | convolution fusion | flops 3221618688 | bytes 11272192 | tf_op jit(solution)/shard_map/dot_general | solution.py:109
  (4 shorter events, 0.0 us)
Async XLA Ops:
  6.5 95.6 %all-gather.9.cloned.1.call-start = ((), (), s32[]{:S(2)}) async-start(), calls=%async_computation | async-start | bytes 6488064 | tf_op jit(solution)/shard_map/all_gather | solution.py:71
  7.3 183.1 %all-gather.13.cloned.1.call-start = ((), (), s32[]{:S(2)}) async-start(), calls=%async_computation.2 | async-start | bytes 6488064 | tf_op jit(solution)/shard_map/all_gather | solution.py:70
  8.0 270.7 %all-gather.11.cloned.1.call-start = ((), (), s32[]{:S(2)}) async-start(), calls=%async_computation.1 | async-start | bytes 6488064 | tf_op jit(solution)/shard_map/all_gather | solution.py:69
  8.7 367.6 %all-gather.19.cloned.1.call-start = ((), (), s32[]{:S(2)}) async-start(), calls=%async_computation.5 | async-start | bytes 8650752 | tf_op jit(solution)/shard_map/all_gather | solution.py:12
  200.0 264.7 %all-gather.17.cloned.1.call-start = ((), (), s32[]{:S(2)}) async-start(), calls=%async_computation.4 | async-start | bytes 6488064 | tf_op jit(solution)/shard_map/all_gather | solution.py:111
  200.6 298.3 %all-gather.15.cloned.1.call-start = ((), (), s32[]{:S(2)}) async-start(), calls=%async_computation.3 | async-start | bytes 4718592 | tf_op jit(solution)/shard_map/all_gather | solution.py:108
  291.3 86.1 %copy-start = (f32[512]{0:T(512)S(1)}, f32[512]{0:T(512)}, u32[]{:S(2)}) copy-start(f32[512]{0:T(512)} %param.16) | copy-start | bytes 6148
Sparse Core Ops, SparseCore 0:
  9.9 92.1 all-gather.8
  104.7 85.6 all-gather.12
  192.9 85.6 all-gather.10
  281.1 95.1 all-gather.18
  378.8 85.8 all-gather.16
  466.3 32.4 all-gather.14
where the time goes:
time: 515 us; the launch traced here: 514 us
  waiting for transfers between devices  424 us (82%)
  matrix products  40.4 us (8%)
  blocking collectives  31.6 us (6%)
  between operations  13.6 us (3%)
    all_gather x1, waiting for transfers between devices, local(): lax.all_gather(content_projector, 'seq', axis=0, tiled=True)  90.6 us
    all_gather x1, waiting for transfers between devices, local(): lax.all_gather(final_projector, 'seq', axis=0, tiled=True)  86.3 us
    all_gather x1, waiting for transfers between devices, entering(): gathered = jax.tree.map(lambda a: lax.all_gather(a, axis), part)  84 us
    all_gather x1, waiting for transfers between devices, local(): lax.all_gather(lookup_projector, 'seq', axis=0, tiled=True)  80.2 us
    all_gather x1, waiting for transfers between devices, local(): lax.all_gather(question_projector, 'seq', axis=0, tiled=True)  46.4 us
    all_gather x1, waiting for transfers between devices, local(): every_head = lax.all_gather(normed, 'tp', axis=1, tiled=True)  34.2 us
    all_gather x1, blocking collectives, entering(): gathered = jax.tree.map(lambda a: lax.all_gather(a, axis), part)  31.6 us
    dot_general x3, matrix products, project_rows(): jnp.dot(event_vectors, shard_rows, preferred_element_type=jnp.float32)  24.4 us
  transfers between devices with their start and end apart: 6, of which 6 were waited for; matrix products, arithmetic and copies ran while one was open for 7% of the time, Pallas kernels for 0%

commit v1 on v0

--- a/solution.py
+++ b/solution.py
@@ -5,6 +5,11 @@
 
 HD = 128
 SPAN_LENGTH = 512
+
+
+def all_by_exchange(block, mesh_axis, dim):
+    outgoing = jnp.stack([block] * lax.axis_size(mesh_axis))
+    return jnp.concatenate(lax.all_to_all(outgoing, mesh_axis, 0, 0), axis=dim)
 
 
 def entering(part, axis, combine, identity):
@@ -107,9 +112,7 @@
     normed = normed.reshape((tok_count, number_of_heads * HD)).astype(jnp.bfloat16)
     every_head = lax.all_gather(normed, "tp", axis=1, tiled=True)
     mixed = jnp.dot(
-        every_head,
-        lax.all_gather(final_projector, "seq", axis=0, tiled=True),
-        preferred_element_type=jnp.float32,
+        every_head, all_by_exchange(final_projector, "seq", 0), preferred_element_type=jnp.float32
     )
     return mixed.astype(jnp.bfloat16)
 

time: 515 us -> 544 us (1.056)
  blocking collectives: 31.6 us -> 203 us
  waiting for transfers between devices: 424 us -> 273 us
    all_gather x1, blocking collectives: 31.6 us -> 203 us  [entering(): gathered = jax.tree.map(lambda a: lax.all_gather(a, axis), part)]
    all_gather x1 -> x0, waiting for transfers between devices: 86.3 us -> none  [local(): lax.all_gather(final_projector, 'seq', axis=0, tiled=True)]
    all_gather x1, waiting for transfers between devices: 84 us -> 35.2 us  [entering(): gathered = jax.tree.map(lambda a: lax.all_gather(a, axis), part)]
    all_gather x1, waiting for transfers between devices: 46.4 us -> 0.02 us  [local(): lax.all_gather(question_projector, 'seq', axis=0, tiled=True)]
    all_gather x1, waiting for transfers between devices: 34.2 us -> 64.6 us  [local(): every_head = lax.all_gather(normed, 'tp', axis=1, tiled=True)]
  transfers between devices with their start and end apart: 6 -> 6, of which waited for: 6 -> 4; matrix products, arithmetic and copies ran while one was open for 7% -> 7% of each run, Pallas kernels for 0% -> 0%
where the time goes in v1:
time: 544 us; the launch traced here: 543 us
  waiting for transfers between devices  273 us (50%)
  blocking collectives  203 us (37%)
  matrix products  41 us (8%)
  between operations  13.3 us (2%)
  starting transfers between devices  5.57 us (1%)
    all_gather x1, blocking collectives, entering(): gathered = jax.tree.map(lambda a: lax.all_gather(a, axis), part)  203 us
    all_gather x1, waiting for transfers between devices, local(): lax.all_gather(content_projector, 'seq', axis=0, tiled=True)  90.6 us
    all_gather x1, waiting for transfers between devices, local(): lax.all_gather(lookup_projector, 'seq', axis=0, tiled=True)  80.2 us
    all_gather x1, waiting for transfers between devices, local(): every_head = lax.all_gather(normed, 'tp', axis=1, tiled=True)  64.6 us
    all_gather x1, waiting for transfers between devices, entering(): gathered = jax.tree.map(lambda a: lax.all_gather(a, axis), part)  35.2 us
    dot_general x3, matrix products, project_rows(): jnp.dot(event_vectors, shard_rows, preferred_element_type=jnp.float32)  25 us
  transfers between devices with their start and end apart: 6, of which 4 were waited for; matrix products, arithmetic and copies ran while one was open for 7% of the time, Pallas kernels for 0%

profile of v1, /device:TPU:1, one launch (start us, length us, event | category | flops | bytes accessed | tf_op | source)
XLA Modules:
  0.0 542.8 jit_solution(9116140395271626068)
XLA Ops:
  6.5 0.0 all-gather.8.cloned.1.call-start
  6.5 0.7 all-gather.8.cloned.1.call-update
  7.3 0.0 all-gather.12.cloned.1.call-start
  7.3 0.7 all-gather.12.cloned.1.call-update
  8.0 0.0 all-gather.10.cloned.1.call-start
  8.1 0.7 all-gather.10.cloned.1.call-update
  8.7 0.0 all-gather.16.cloned.1.call-start
  8.8 0.8 broadcast_subtract_fusion
  9.6 1.2 reduce-window.6
  10.8 0.2 slice_reduce_fusion
  10.9 0.2 reduce-window.9
  11.1 0.1 add_bitcast_fusion
  11.2 0.2 slice_reduce_fusion.1
  11.4 0.1 subtract_exponential_fusion
  11.5 90.6 %all-gather.8.cloned.1.call-done = bf16[6144,512]{1,0:T(8,128)(2,1)} async-done(((bf16[192,512]{1,0:T(8,128)(2,1)}), bf16[6144,512]{1,0:T(8,128)(2,1)}) %all-gather.8.cloned.1.call-update) | async-done | bytes 6291472 | tf_op jit(solution)/shard_map/all_gather | solution.py:76
  102.1 8.1 %convolution_convert_fusion.1 = bf16[512,512]{0,1:T(8,128)(2,1)S(1)} fusion(bf16[512,6144]{1,0:T(8,128)(2,1)} %param.10, bf16[6144,512]{1,0:T(8,128)(2,1)} %all-gather.8.cloned.1.call-done), kind=kOutput, calls=%fused_computation.18 | convolution fusion | flops 3221487616 | bytes 13107200 | tf_op jit(solution)/shard_map/dot_general | solution.py:72
  110.2 0.0 copy-start
  110.2 80.2 %all-gather.12.cloned.1.call-done = bf16[6144,512]{1,0:T(8,128)(2,1)} async-done(((bf16[192,512]{1,0:T(8,128)(2,1)}), bf16[6144,512]{1,0:T(8,128)(2,1)}) %all-gather.12.cloned.1.call-update) | async-done | bytes 6291472 | tf_op jit(solution)/shard_map/all_gather | solution.py:75
  190.4 8.2 %multiply_convert_fusion.1 = bf16[512,512]{0,1:T(8,128)(2,1)S(1)} fusion(bf16[512,6144]{1,0:T(8,128)(2,1)} %param.10, bf16[6144,512]{1,0:T(8,128)(2,1)} %all-gather.12.cloned.1.call-done), kind=kOutput, calls=%fused_computation.27 | convolution fusion | flops 3222536192 | bytes 13107200 | tf_op jit(solution)/shard_map/dot_general | solution.py:72
  198.6 1.4 convolution_add_fusion.1
  199.9 0.0 all-gather.16.cloned.1.call-update
  200.0 0.0 copy-done
  200.0 3.3 stack.2
  203.3 5.4 all-to-all-start
  208.7 0.0 all-gather.14.cloned.1.call-start
  208.7 202.9 %all-gather.1 = f32[32,1,4]{2,1,0:T(1,128)S(1)} all-gather(f32[1,1,4]{2,1,0:T(1,128)S(1)} %bitcast.70), channel_id=1, replica_groups=mesh['seq'=32,'tp'=8] {'seq'}, dimensions={0}, use_global_device_ids=true | all-gather | bytes 528 | tf_op jit(solution)/shard_map/all_gather | solution.py:17
  411.7 0.1 iota_compare_fusion
  411.7 0.0 all-gather.10.cloned.1.call-done
  411.8 8.7 %multiply_convert_fusion.2 = bf16[512,512]{0,1:T(8,128)(2,1)S(1)} fusion(bf16[512,6144]{1,0:T(8,128)(2,1)} %param.10, bf16[6144,512]{1,0:T(8,128)(2,1)} %all-gather.10.cloned.1.call-done), kind=kOutput, calls=%fused_computation.28 | convolution fusion | flops 3222536192 | bytes 13107200 | tf_op jit(solution)/shard_map/dot_general | solution.py:72
  420.5 0.7 fusion.23
  421.3 3.7 fusion
  425.0 0.0 copy-start.1
  425.0 1.0 fusion.12
  426.0 35.2 %all-gather.16.cloned.1.call-done = f32[128,128,128]{2,1,0:T(8,128)} async-done(((f32[4,128,128]{2,1,0:T(8,128)}), f32[128,128,128]{2,1,0:T(8,128)}) %all-gather.16.cloned.1.call-update) | async-done | bytes 8388624 | tf_op jit(solution)/shard_map/all_gather | solution.py:17
  461.2 0.2 while.3
  461.5 0.7 multiply_reduce_fusion
  462.2 0.0 copy-done.1
  462.2 0.9 multiply_convert_fusion
  463.2 0.0 all-gather.14.cloned.1.call-update
  463.2 0.0 all-to-all-done
  463.2 64.6 %all-gather.14.cloned.1.call-done = bf16[512,4096]{0,1:T(8,128)(2,1)} async-done(((bf16[512,512]{0,1:T(8,128)(2,1)}), bf16[512,4096]{0,1:T(8,128)(2,1)}) %all-gather.14.cloned.1.call-update) | async-done | bytes 4194320 | tf_op jit(solution)/shard_map/all_gather | solution.py:113
  527.9 8.4 %convolution_convert_fusion = bf16[512,768]{1,0:T(8,128)(2,1)} fusion(bf16[512,4096]{0,1:T(8,128)(2,1)} %all-gather.14.cloned.1.call-done, bf16[4096,768]{1,0:T(8,128)(2,1)} %bitcast.13), kind=kOutput, calls=%fused_computation.12 | convolution fusion | flops 3221618688 | bytes 11272192 | tf_op jit(solution)/shard_map/dot_general | solution.py:114
  (4 shorter events, 0.0 us)
Async XLA Ops:
  6.5 95.6 %all-gather.8.cloned.1.call-start = ((), (), s32[]{:S(2)}) async-start(), calls=%async_computation.1 | async-start | bytes 6488064 | tf_op jit(solution)/shard_map/all_gather | solution.py:76
  7.3 183.1 %all-gather.12.cloned.1.call-start = ((), (), s32[]{:S(2)}) async-start(), calls=%async_computation.3 | async-start | bytes 6488064 | tf_op jit(solution)/shard_map/all_gather | solution.py:75
  8.0 403.8 %all-gather.10.cloned.1.call-start = ((), (), s32[]{:S(2)}) async-start(), calls=%async_computation.2 | async-start | bytes 6488064 | tf_op jit(solution)/shard_map/all_gather | solution.py:74
  8.7 452.5 %all-gather.16.cloned.1.call-start = ((), (), s32[]{:S(2)}) async-start(), calls=%async_computation.5 | async-start | bytes 8650752 | tf_op jit(solution)/shard_map/all_gather | solution.py:17
  110.2 89.8 %copy-start = (bf16[128,768]{1,0:T(8,128)(2,1)S(1)}, bf16[128,768]{1,0:T(8,128)(2,1)}, u32[]{:S(2)}) copy-start(bf16[128,768]{1,0:T(8,128)(2,1)} %param.17) | copy-start | bytes 589828
  203.3 260.0 %all-to-all-start = ((bf16[32,128,768]{2,1,0:T(8,128)(2,1)}), bf16[32,128,768]{2,1,0:T(8,128)(2,1)}, u32[]{:S(2)}, u32[]{:S(2)}) async-start(bf16[32,128,768]{2,1,0:T(8,128)(2,1)} %stack.2), calls=%async_computation | async-start | bytes 12582912 | tf_op jit(solution)/shard_map/all_to_all | solution.py:12
  208.7 319.2 %all-gather.14.cloned.1.call-start = ((), (), s32[]{:S(2)}) async-start(), calls=%async_computation.4 | async-start | bytes 4718592 | tf_op jit(solution)/shard_map/all_gather | solution.py:113
  425.0 37.3 %copy-start.1 = (f32[512]{0:T(512)S(1)}, f32[512]{0:T(512)}, u32[]{:S(2)}) copy-start(f32[512]{0:T(512)} %param.16) | copy-start | bytes 6148
Sparse Core Ops, SparseCore 0:
  9.9 92.1 all-gather.7
  104.7 85.6 all-gather.11
  192.9 161.2 all-gather.9
  356.7 104.4 all-gather.15
  463.3 64.4 all-gather.13
